TPU v7x, 32 devices: a whole 2x2x4 slice. The times are simulated.
32 devices in a mesh: mod: 4 (over z), frm: 2 (over x), ori: 4 (over y, core).
Axes of the slice: x: 2, y: 2, z: 4, core: 2. Of those that a mesh axis runs over, the one named last changes fastest.
Arguments:
- counts: int32 [512, 128, 128], P(('frm', 'ori'), 'mod'), may hold values from 0 to 8
- slice_codes: int32 [4096, 128, 128], P('ori', ('mod', 'frm')), may hold values from 0 to 2047
- pixel_mask: int32 [128, 128], P('mod'), may hold values 0 or 1
Outputs:
- log_posterior: float32 [2, 256, 4096], P('frm', 'mod', 'ori')
All inputs are finite; a program needn't handle non-finite values. No bound on the sum of `pixel_mask` on one device may be relied on, other than what follows from the above.
Results may differ from a plain program's by a relative error of at most 0.0024.
Values may be sent and summed in bfloat16 or wider, within the bound.
A program may use at most 64 MiB of HBM per device.

v0:
```python
import math
import jax
import jax.numpy as jnp
from jax import lax
from jax.sharding import PartitionSpec as P

PASSES = 8
TIME_STEP = 0.2
EDGE_SCALE = 2.0
LOG_FLOOR = -7.0
CODE_STEP = 1.0 / 256.0


def extended(x, sides, width):
    for axis, dim in sides:
        peers, length = (lax.axis_size(axis), x.shape[dim])
        up = [(i, (i + 1) % peers) for i in range(peers - 1)]
        down = [(j, i) for i, j in up]
        last = lax.slice_in_dim(x, length - width, length, axis=dim)
        leading = lax.slice_in_dim(x, 0, width, axis=dim)
        before = lax.ppermute(last, axis, up)
        after = lax.ppermute(leading, axis, down)
        x = jnp.concatenate([before, x, after], axis=dim)
    return x


def conduct(difference):
    ratio = difference / EDGE_SCALE
    return difference / (1.0 + ratio * ratio)


def relax_once(padded):
    centre = padded[:, 1:-1, :]
    column_pad = jnp.zeros((centre.shape[0], centre.shape[1], 1), jnp.float32)
    left_side = jnp.concatenate([column_pad, centre[:, :, :-1]], axis=2)
    right_side = jnp.concatenate([centre[:, :, 1:], column_pad], axis=2)
    flux_sum = conduct(padded[:, :-2, :] - centre) + conduct(padded[:, 2:, :] - centre)
    flux_sum = flux_sum + conduct(left_side - centre) + conduct(right_side - centre)
    return centre + TIME_STEP * flux_sum


def body(counts, slice_codes, pixel_mask):
    intensity = counts.astype(jnp.float32)
    module_rows = intensity.shape[1]
    total_rows = module_rows * lax.axis_size("mod")
    first_row = lax.axis_index("mod") * module_rows
    row_ids = first_row - 1 + lax.broadcasted_iota(jnp.int32, (1, module_rows + 2, 1), 1)
    inside = ((row_ids >= 0) & (row_ids < total_rows)).astype(jnp.float32)
    for pair_index in range(PASSES // 2):
        padded = extended(intensity, (("mod", 1),), 2)
        widened = relax_once(padded) * inside
        intensity = relax_once(widened)
    cleaned = intensity.astype(jnp.bfloat16) * pixel_mask.astype(jnp.bfloat16)[None]
    gathered = lax.all_gather(cleaned, "ori", axis=0, tiled=True)
    log_slices = (LOG_FLOOR + slice_codes.astype(jnp.float32) * CODE_STEP).astype(jnp.bfloat16)
    band_rows = log_slices.shape[1]
    own_mask = lax.dynamic_slice_in_dim(
        pixel_mask, lax.axis_index("frm") * band_rows, band_rows, 0
    ).astype(jnp.float32)
    local_totals = jnp.sum(jnp.exp(log_slices.astype(jnp.float32)) * own_mask[None], axis=(1, 2))
    module_totals = lax.psum(local_totals, "frm")
    product = lax.dot_general(
        gathered,
        lax.all_gather(log_slices, "frm", axis=1, tiled=True),
        (((1, 2), (1, 2)), ((), ())),
        preferred_element_type=jnp.float32,
    )
    partial_value = product - module_totals[None, :]
    scale_factor = 1.0 / math.sqrt(module_rows * lax.axis_size("mod") * intensity.shape[2])
    summed = lax.psum(partial_value, "mod")
    share_rows = summed.shape[0] // lax.axis_size("mod")
    own_rows = lax.dynamic_slice_in_dim(summed, lax.axis_index("mod") * share_rows, share_rows, 0)
    scores = own_rows * scale_factor
    peaks = lax.pmax(jnp.max(scores, axis=1), "ori")
    masses = lax.psum(jnp.sum(jnp.exp(scores - peaks[:, None]), axis=1), "ori")
    log_posterior = scores - (peaks + jnp.log(masses))[:, None]
    return log_posterior[None]


def solution(mesh):
    in_specs = (P(("frm", "ori"), "mod", None), P("ori", ("mod", "frm"), None), P("mod", None))
    out_specs = P("frm", "mod", "ori")
    return jax.shard_map(body, mesh=mesh, in_specs=in_specs, out_specs=out_specs, check_vma=False)
```

profile of v0, /device:TPU:0, one launch (start us, length us, event | category | flops | bytes accessed | tf_op | source)
XLA Modules:
  0.0 270.0 jit_solution(14299693022543329256)
XLA Ops:
  6.5 1.8 copy_convert_fusion.1
  8.4 5.0 %collective-permute-start = (f32[64,2,128]{2,0,1:T(8,128)S(1)}, f32[64,2,128]{2,0,1:T(8,128)S(1)}, u32[]{:S(2)}, u32[]{:S(2)}) collective-permute-start(f32[64,2,128]{2,0,1:T(8,128)S(1)} %get-tuple-element.29), channel_id=1, source_target_pairs={{0,8},{8,16},{16,24},{1,9},{9,17},{17,25},{2,10},{10,18},{18,26},{... | collective-permute-start | bytes 196616 | tf_op jit(solution)/shard_map/ppermute | solution.py:21
  13.4 1.3 collective-permute-start.1
  15.2 4.3 %collective-permute-done.1 = f32[64,2,128]{2,0,1:T(8,128)S(1)} collective-permute-done((f32[64,2,128]{2,0,1:T(8,128)S(1)}, f32[64,2,128]{2,0,1:T(8,128)S(1)}, u32[]{:S(2)}, u32[]{:S(2)}) %collective-permute-start.1) | collective-permute-done | bytes 65568 | tf_op jit(solution)/shard_map/ppermute | solution.py:22
  20.0 1.2 add_multiply_fusion.3
  21.6 1.1 multiply_add_fusion.2
  22.7 3.5 %collective-permute-start.2 = (f32[64,2,128]{2,0,1:T(8,128)S(1)}, f32[64,2,128]{2,0,1:T(8,128)S(1)}, u32[]{:S(2)}, u32[]{:S(2)}) collective-permute-start(f32[64,2,128]{2,0,1:T(8,128)S(1)} %get-tuple-element.27), channel_id=1, source_target_pairs={{0,8},{8,16},{16,24},{1,9},{9,17},{17,25},{2,10},{10,18},{18,26},{... | collective-permute-start | bytes 196616 | tf_op jit(solution)/shard_map/ppermute | solution.py:21
  26.2 1.3 collective-permute-start.3
  28.1 4.3 %collective-permute-done.3 = f32[64,2,128]{2,0,1:T(8,128)S(1)} collective-permute-done((f32[64,2,128]{2,0,1:T(8,128)S(1)}, f32[64,2,128]{2,0,1:T(8,128)S(1)}, u32[]{:S(2)}, u32[]{:S(2)}) %collective-permute-start.3) | collective-permute-done | bytes 65568 | tf_op jit(solution)/shard_map/ppermute | solution.py:22
  32.9 1.2 add_multiply_fusion.2
  34.5 1.1 multiply_add_fusion.1
  35.6 3.5 %collective-permute-start.4 = (f32[64,2,128]{2,0,1:T(8,128)S(1)}, f32[64,2,128]{2,0,1:T(8,128)S(1)}, u32[]{:S(2)}, u32[]{:S(2)}) collective-permute-start(f32[64,2,128]{2,0,1:T(8,128)S(1)} %get-tuple-element.25), channel_id=1, source_target_pairs={{0,8},{8,16},{16,24},{1,9},{9,17},{17,25},{2,10},{10,18},{18,26},{... | collective-permute-start | bytes 196616 | tf_op jit(solution)/shard_map/ppermute | solution.py:21
  39.1 1.3 collective-permute-start.5
  41.0 4.3 %collective-permute-done.5 = f32[64,2,128]{2,0,1:T(8,128)S(1)} collective-permute-done((f32[64,2,128]{2,0,1:T(8,128)S(1)}, f32[64,2,128]{2,0,1:T(8,128)S(1)}, u32[]{:S(2)}, u32[]{:S(2)}) %collective-permute-start.5) | collective-permute-done | bytes 65568 | tf_op jit(solution)/shard_map/ppermute | solution.py:22
  45.8 1.2 add_multiply_fusion.1
  47.4 1.1 multiply_add_fusion
  48.6 1.9 collective-permute-start.6
  50.5 1.5 collective-permute-start.7
  52.4 4.3 %collective-permute-done.7 = f32[64,2,128]{2,0,1:T(8,128)S(1)} collective-permute-done((f32[64,2,128]{2,0,1:T(8,128)S(1)}, f32[64,2,128]{2,0,1:T(8,128)S(1)}, u32[]{:S(2)}, u32[]{:S(2)}) %collective-permute-start.7) | collective-permute-done | bytes 65568 | tf_op jit(solution)/shard_map/ppermute | solution.py:22
  57.1 1.2 add_multiply_fusion
  58.7 2.0 fusion.4
  60.8 7.8 %multiply_reduce_fusion = (f32[1024]{0:T(1024)S(1)}, bf16[1024,16,128]{2,0,1:T(8,128)(2,1)}) fusion(f32[16,128]{1,0:T(8,128)S(1)} %dynamic-slice_convert_fusion, s32[1024,16,128]{2,1,0:T(8,128)} %param.4), kind=kLoop, calls=%fused_computation.4 | loop fusion | flops 14679040 | bytes 12595200 | tf_op jit(solution)/shard_map/reduce_sum | solution.py:60
  68.6 4.9 %psum.21 = f32[1024]{0:T(1024)S(1)} all-reduce(f32[1024]{0:T(1024)S(1)} %get-tuple-element.5), channel_id=1, replica_groups=mesh['mod'=4,'frm'=2,'ori'=4] {'frm'}, use_global_device_ids=true, to_apply=%region_1.0 | all-reduce | flops 1024 | bytes 8192 | tf_op jit(solution)/shard_map/psum | solution.py:61
  73.6 8.1 %all-gather.3.cloned.1.call-done = bf16[256,32,128]{2,0,1:T(8,128)(2,1)} async-done(((bf16[64,32,128]{2,0,1:T(8,128)(2,1)}), bf16[256,32,128]{2,0,1:T(8,128)(2,1)}) %all-gather.3.cloned.1.call-update) | async-done | bytes 2097168 | tf_op jit(solution)/shard_map/all_gather | solution.py:54
  81.7 105.5 %all-gather.5.cloned.1.call-done = bf16[1024,32,128]{2,0,1:T(8,128)(2,1)} async-done(((bf16[1024,16,128]{2,0,1:T(8,128)(2,1)}), bf16[1024,32,128]{2,0,1:T(8,128)(2,1)}) %all-gather.5.cloned.1.call-update) | async-done | bytes 8388624 | tf_op jit(solution)/shard_map/all_gather | solution.py:64
  187.2 7.4 %fusion.3 = f32[256,1024]{1,0:T(8,128)} fusion(bf16[256,32,128]{2,0,1:T(8,128)(2,1)} %all-gather.3.cloned.1.call-done, bf16[1024,32,128]{2,0,1:T(8,128)(2,1)} %all-gather.5.cloned.1.call-done, f32[1024]{0:T(1024)S(1)} %psum.21), kind=kOutput, calls=%fused_computation.6 | convolution fusion | flops 2147745792 | bytes 11538432 | tf_op jit(solution)/shard_map/dot_general | solution.py:62
  194.7 52.1 %all-reduce.18.cloned.1.call-done = f32[256,1024]{1,0:T(8,128)} async-done(((f32[256,1024]{1,0:T(8,128)}), f32[256,1024]{1,0:T(8,128)}) %all-reduce.18.cloned.1.call-update) | async-done | bytes 1048592 | tf_op jit(solution)/shard_map/psum | solution.py:70
  246.7 1.1 fusion.5
  247.8 6.9 %pmax.7 = f32[64]{0:T(128)S(1)} all-reduce(f32[64]{0:T(128)S(1)} %fusion.5), channel_id=1, replica_groups=mesh['mod'=4,'frm'=2,'ori'=4] {'ori'}, use_global_device_ids=true, to_apply=%region_4.0 | all-reduce | flops 64 | bytes 512 | tf_op jit(solution)/shard_map/pmax | solution.py:74
  254.7 1.2 exponential_reduce_fusion
  255.8 5.9 %psum.23 = f32[64]{0:T(128)S(1)} all-reduce(f32[64]{0:T(128)S(1)} %exponential_reduce_fusion), channel_id=1, replica_groups=mesh['mod'=4,'frm'=2,'ori'=4] {'ori'}, use_global_device_ids=true, to_apply=%region_6.0 | all-reduce | flops 64 | bytes 512 | tf_op jit(solution)/shard_map/psum | solution.py:75
  261.8 1.7 subtract_bitcast_fusion
  (32 shorter events, 5.8 us)
Async XLA Ops:
  6.5 75.1 %all-gather.3.cloned.1.call-start = ((), (), s32[]{:S(2)}) async-start(), calls=%async_computation | async-start | bytes 2621440 | tf_op jit(solution)/shard_map/all_gather | solution.py:54
  8.4 6.9 %collective-permute-start = (f32[64,2,128]{2,0,1:T(8,128)S(1)}, f32[64,2,128]{2,0,1:T(8,128)S(1)}, u32[]{:S(2)}, u32[]{:S(2)}) collective-permute-start(f32[64,2,128]{2,0,1:T(8,128)S(1)} %get-tuple-element.29), channel_id=1, source_target_pairs={{0,8},{8,16},{16,24},{1,9},{9,17},{17,25},{2,10},{10,18},{18,26},{... | collective-permute-start | bytes 196616 | tf_op jit(solution)/shard_map/ppermute | solution.py:21
  13.4 6.2 %collective-permute-start.1 = (f32[64,2,128]{2,0,1:T(8,128)S(1)}, f32[64,2,128]{2,0,1:T(8,128)S(1)}, u32[]{:S(2)}, u32[]{:S(2)}) collective-permute-start(f32[64,2,128]{2,0,1:T(8,128)S(1)} %get-tuple-element.30), channel_id=1, source_target_pairs={{8,0},{16,8},{24,16},{9,1},{17,9},{25,17},{10,2},{18,10},{26,18},{... | collective-permute-start | bytes 196616 | tf_op jit(solution)/shard_map/ppermute | solution.py:22
  22.7 5.4 %collective-permute-start.2 = (f32[64,2,128]{2,0,1:T(8,128)S(1)}, f32[64,2,128]{2,0,1:T(8,128)S(1)}, u32[]{:S(2)}, u32[]{:S(2)}) collective-permute-start(f32[64,2,128]{2,0,1:T(8,128)S(1)} %get-tuple-element.27), channel_id=1, source_target_pairs={{0,8},{8,16},{16,24},{1,9},{9,17},{17,25},{2,10},{10,18},{18,26},{... | collective-permute-start | bytes 196616 | tf_op jit(solution)/shard_map/ppermute | solution.py:21
  26.2 6.2 %collective-permute-start.3 = (f32[64,2,128]{2,0,1:T(8,128)S(1)}, f32[64,2,128]{2,0,1:T(8,128)S(1)}, u32[]{:S(2)}, u32[]{:S(2)}) collective-permute-start(f32[64,2,128]{2,0,1:T(8,128)S(1)} %get-tuple-element.28), channel_id=1, source_target_pairs={{8,0},{16,8},{24,16},{9,1},{17,9},{25,17},{10,2},{18,10},{26,18},{... | collective-permute-start | bytes 196616 | tf_op jit(solution)/shard_map/ppermute | solution.py:22
  35.6 5.4 %collective-permute-start.4 = (f32[64,2,128]{2,0,1:T(8,128)S(1)}, f32[64,2,128]{2,0,1:T(8,128)S(1)}, u32[]{:S(2)}, u32[]{:S(2)}) collective-permute-start(f32[64,2,128]{2,0,1:T(8,128)S(1)} %get-tuple-element.25), channel_id=1, source_target_pairs={{0,8},{8,16},{16,24},{1,9},{9,17},{17,25},{2,10},{10,18},{18,26},{... | collective-permute-start | bytes 196616 | tf_op jit(solution)/shard_map/ppermute | solution.py:21
  39.1 6.2 %collective-permute-start.5 = (f32[64,2,128]{2,0,1:T(8,128)S(1)}, f32[64,2,128]{2,0,1:T(8,128)S(1)}, u32[]{:S(2)}, u32[]{:S(2)}) collective-permute-start(f32[64,2,128]{2,0,1:T(8,128)S(1)} %get-tuple-element.26), channel_id=1, source_target_pairs={{8,0},{16,8},{24,16},{9,1},{17,9},{25,17},{10,2},{18,10},{26,18},{... | collective-permute-start | bytes 196616 | tf_op jit(solution)/shard_map/ppermute | solution.py:22
  47.4 4.5 %copy-start = (s32[32,128]{1,0:T(8,128)S(1)}, s32[32,128]{1,0:T(8,128)}, u32[]{:S(2)}) copy-start(s32[32,128]{1,0:T(8,128)} %param.5) | copy-start | bytes 49156
  48.6 3.8 %collective-permute-start.6 = (f32[64,2,128]{2,0,1:T(8,128)S(1)}, f32[64,2,128]{2,0,1:T(8,128)S(1)}, u32[]{:S(2)}, u32[]{:S(2)}) collective-permute-start(f32[64,2,128]{2,0,1:T(8,128)S(1)} %get-tuple-element.23), channel_id=1, source_target_pairs={{0,8},{8,16},{16,24},{1,9},{9,17},{17,25},{2,10},{10,18},{18,26},{... | collective-permute-start | bytes 196616 | tf_op jit(solution)/shard_map/ppermute | solution.py:21
  50.5 6.2 %collective-permute-start.7 = (f32[64,2,128]{2,0,1:T(8,128)S(1)}, f32[64,2,128]{2,0,1:T(8,128)S(1)}, u32[]{:S(2)}, u32[]{:S(2)}) collective-permute-start(f32[64,2,128]{2,0,1:T(8,128)S(1)} %get-tuple-element.24), channel_id=1, source_target_pairs={{8,0},{16,8},{24,16},{9,1},{17,9},{25,17},{10,2},{18,10},{26,18},{... | collective-permute-start | bytes 196616 | tf_op jit(solution)/shard_map/ppermute | solution.py:22
  60.7 126.5 %all-gather.5.cloned.1.call-start = ((), (), s32[]{:S(2)}) async-start(), calls=%async_computation.1 | async-start | bytes 12582912 | tf_op jit(solution)/shard_map/all_gather | solution.py:64
  68.6 178.1 %all-reduce.18.cloned.1.call-start = ((), (), s32[]{:S(2)}) async-start(), calls=%async_computation.2 | async-start | bytes 2097152 | tf_op jit(solution)/shard_map/psum | solution.py:70
Sparse Core Ops, SparseCore 0:
  60.9 20.7 all-gather.2
  83.2 103.9 all-gather.4
  194.8 51.8 all-reduce.17
where the time goes:
time: 271 us; the launch traced here: 270 us
  waiting for transfers between devices  185 us (68%)
  other arithmetic  24.2 us (9%)
  starting transfers between devices  19.3 us (7%)
  blocking collectives  17.7 us (7%)
  between operations  13.4 us (5%)
  matrix products  7.45 us (3%)
  local copies, waits for them, and re-layouts  3.11 us (1%)
    all_gather x1, waiting for transfers between devices, body(): lax.all_gather(log_slices, 'frm', axis=1, tiled=True)  106 us
    psum x1, waiting for transfers between devices, body(): summed = lax.psum(partial_value, 'mod')  52.1 us
    ppermute x4, waiting for transfers between devices, extended(): after = lax.ppermute(leading, axis, down)  17.1 us
    ppermute x4, starting transfers between devices, extended(): before = lax.ppermute(last, axis, up)  13.8 us
    all_gather x1, waiting for transfers between devices, body(): gathered = lax.all_gather(cleaned, 'ori', axis=0, tiled=True)  8.08 us
    reduce_sum x1, other arithmetic, body(): jnp.sum(jnp.exp(log_slices.astype(jnp.float32)) * own_mask[None], axis=(1...  7.77 us
    dot_general x1, matrix products, body(): lax.dot_general(gathered, lax.all_gather(log_slices, 'frm', axis=1, tiled...  7.45 us
    pmax x1, blocking collectives, body(): peaks = lax.pmax(jnp.max(scores, axis=1), 'ori')  6.85 us
  transfers between devices with their start and end apart: 11, of which 11 were waited for; matrix products, arithmetic and copies ran while one was open for 3% of the time, Pallas kernels for 0%

commit v1 on v0

--- a/solution.py
+++ b/solution.py
@@ -9,6 +9,28 @@
 EDGE_SCALE = 2.0
 LOG_FLOOR = -7.0
 CODE_STEP = 1.0 / 256.0
+
+
+def laid_out(pieces, dim):
+    pieces = jnp.moveaxis(pieces, 0, dim)
+    shape = pieces.shape
+    return pieces.reshape(*shape[:dim], shape[dim] * shape[dim + 1], *shape[dim + 2 :])
+
+
+def doubled(array, axis):
+    size = lax.axis_size(axis)
+    blocks = array[None]
+    for level in range(size.bit_length() - 1):
+        bit = 1 << level
+        other = lax.ppermute(blocks, axis, [(i, i ^ bit) for i in range(size)])
+        both = jnp.stack([blocks, other])
+        upper = lax.axis_index(axis) >> level & 1
+        blocks = jnp.where(upper == 0, both, both[::-1]).reshape(-1, *array.shape)
+    return blocks
+
+
+def gather_by_bits(array, axis, dim):
+    return laid_out(doubled(array, axis), dim)
 
 
 def extended(x, sides, width):
@@ -61,7 +83,7 @@
     module_totals = lax.psum(local_totals, "frm")
     product = lax.dot_general(
         gathered,
-        lax.all_gather(log_slices, "frm", axis=1, tiled=True),
+        gather_by_bits(log_slices, "frm", 1),
         (((1, 2), (1, 2)), ((), ())),
         preferred_element_type=jnp.float32,
     )

time: 271 us -> 242 us (0.89)
  waiting for transfers between devices: 185 us -> 66.6 us
  blocking collectives: 17.7 us -> 82.7 us
  other arithmetic: 24.2 us -> 42.5 us
  starting transfers between devices: 19.3 us -> 23.4 us
    all_gather x1 -> x0, waiting for transfers between devices: 106 us -> none  [body(): lax.all_gather(log_slices, 'frm', axis=1, tiled=True)]
    psum x1, blocking collectives: 4.94 us -> 69.9 us  [body(): module_totals = lax.psum(local_totals, 'frm')]
    select_n x0 -> x1, other arithmetic: none -> 11.1 us  [doubled(): blocks = jnp.where(upper == 0, both, both[::-1]).reshape(-1, *array.shape)]
    all_gather x1, waiting for transfers between devices: 8.08 us -> 0.01 us  [body(): gathered = lax.all_gather(cleaned, 'ori', axis=0, tiled=True)]
    another operation x0 -> x1, other arithmetic: none -> 7.42 us  [doubled(): both = jnp.stack([blocks, other])]
    ppermute x4, waiting for transfers between devices: 17.1 us -> 12.8 us  [extended(): after = lax.ppermute(leading, axis, down)]
  transfers between devices with their start and end apart: 11 -> 11, of which waited for: 11 -> 7; matrix products, arithmetic and copies ran while one was open for 3% -> 14% of each run, Pallas kernels for 0% -> 0%
where the time goes in v1:
time: 242 us
  blocking collectives  82.7 us (34%)
  waiting for transfers between devices  66.6 us (28%)
  other arithmetic  42.5 us (18%)
  starting transfers between devices  23.4 us (10%)
  between operations  13.7 us (6%)
  matrix products  9.63 us (4%)
  local copies, waits for them, and re-layouts  3.18 us (1%)
    psum x1, blocking collectives, body(): module_totals = lax.psum(local_totals, 'frm')  69.9 us
    psum x1, waiting for transfers between devices, body(): summed = lax.psum(partial_value, 'mod')  52.1 us
    ppermute x4, starting transfers between devices, extended(): before = lax.ppermute(last, axis, up)  16.5 us
    ppermute x4, waiting for transfers between devices, extended(): after = lax.ppermute(leading, axis, down)  12.8 us
    select_n x1, other arithmetic, doubled(): blocks = jnp.where(upper == 0, both, both[::-1]).reshape(-1, *array.shape)  11.1 us
    dot_general x1, matrix products, body(): lax.dot_general(gathered, gather_by_bits(log_slices, 'frm', 1), (((1, 2),...  9.63 us
    reduce_sum x1, other arithmetic, body(): jnp.sum(jnp.exp(log_slices.astype(jnp.float32)) * own_mask[None], axis=(1...  7.48 us
    another operation x1, other arithmetic, doubled(): both = jnp.stack([blocks, other])  7.42 us
  transfers between devices with their start and end apart: 11, of which 7 were waited for; matrix products, arithmetic and copies ran while one was open for 14% of the time, Pallas kernels for 0%

profile of v1, /device:TPU:0, one launch (start us, length us, event | category | flops | bytes accessed | tf_op | source)
XLA Modules:
  0.0 241.6 jit_solution(12918103787345356566)
XLA Ops:
  6.5 1.8 copy_convert_fusion
  8.4 5.0 %collective-permute-start = (f32[64,2,128]{2,0,1:T(8,128)S(1)}, f32[64,2,128]{2,0,1:T(8,128)S(1)}, u32[]{:S(2)}, u32[]{:S(2)}) collective-permute-start(f32[64,2,128]{2,0,1:T(8,128)S(1)} %get-tuple-element.30), channel_id=1, source_target_pairs={{0,8},{8,16},{16,24},{1,9},{9,17},{17,25},{2,10},{10,18},{18,26},{... | collective-permute-start | bytes 196616 | tf_op jit(solution)/shard_map/ppermute | solution.py:43
  13.4 1.3 collective-permute-start.1
  15.2 4.3 %collective-permute-done.1 = f32[64,2,128]{2,0,1:T(8,128)S(1)} collective-permute-done((f32[64,2,128]{2,0,1:T(8,128)S(1)}, f32[64,2,128]{2,0,1:T(8,128)S(1)}, u32[]{:S(2)}, u32[]{:S(2)}) %collective-permute-start.1) | collective-permute-done | bytes 65568 | tf_op jit(solution)/shard_map/ppermute | solution.py:44
  20.0 1.2 add_multiply_fusion.3
  21.6 1.1 multiply_add_fusion.2
  22.8 3.5 %collective-permute-start.2 = (f32[64,2,128]{2,0,1:T(8,128)S(1)}, f32[64,2,128]{2,0,1:T(8,128)S(1)}, u32[]{:S(2)}, u32[]{:S(2)}) collective-permute-start(f32[64,2,128]{2,0,1:T(8,128)S(1)} %get-tuple-element.28), channel_id=1, source_target_pairs={{0,8},{8,16},{16,24},{1,9},{9,17},{17,25},{2,10},{10,18},{18,26},{... | collective-permute-start | bytes 196616 | tf_op jit(solution)/shard_map/ppermute | solution.py:43
  26.3 1.3 collective-permute-start.3
  28.1 4.3 %collective-permute-done.3 = f32[64,2,128]{2,0,1:T(8,128)S(1)} collective-permute-done((f32[64,2,128]{2,0,1:T(8,128)S(1)}, f32[64,2,128]{2,0,1:T(8,128)S(1)}, u32[]{:S(2)}, u32[]{:S(2)}) %collective-permute-start.3) | collective-permute-done | bytes 65568 | tf_op jit(solution)/shard_map/ppermute | solution.py:44
  33.0 1.2 add_multiply_fusion.2
  34.6 1.1 multiply_add_fusion.1
  35.7 3.5 %collective-permute-start.4 = (f32[64,2,128]{2,0,1:T(8,128)S(1)}, f32[64,2,128]{2,0,1:T(8,128)S(1)}, u32[]{:S(2)}, u32[]{:S(2)}) collective-permute-start(f32[64,2,128]{2,0,1:T(8,128)S(1)} %get-tuple-element.26), channel_id=1, source_target_pairs={{0,8},{8,16},{16,24},{1,9},{9,17},{17,25},{2,10},{10,18},{18,26},{... | collective-permute-start | bytes 196616 | tf_op jit(solution)/shard_map/ppermute | solution.py:43
  39.2 1.5 collective-permute-start.5
  40.7 7.5 %multiply_reduce_fusion = (f32[1024]{0:T(1024)S(1)}, bf16[1,1024,16,128]{3,2,1,0:T(8,128)(2,1)}, bf16[1,1,1024,16,128]{4,3,0,2,1:T(8,128)(2,1)}) fusion(f32[16,128]{1,0:T(8,128)S(1)} %dynamic-slice_convert_fusion, s32[1024,16,128]{2,1,0:T(8,128)S(1)} %bitcast.21), kind=kLoop, calls=%fused_computation.4 | loop fusion | flops 14679040 | bytes 16789504 | tf_op jit(solution)/shard_map/reduce_sum | solution.py:82
  48.2 1.5 collective-permute-start.8
  50.2 1.2 add_multiply_fusion.1
  51.8 1.1 multiply_add_fusion
  52.9 4.5 %collective-permute-start.6 = (f32[64,2,128]{2,0,1:T(8,128)S(1)}, f32[64,2,128]{2,0,1:T(8,128)S(1)}, u32[]{:S(2)}, u32[]{:S(2)}) collective-permute-start(f32[64,2,128]{2,0,1:T(8,128)S(1)} %get-tuple-element.24), channel_id=1, source_target_pairs={{0,8},{8,16},{16,24},{1,9},{9,17},{17,25},{2,10},{10,18},{18,26},{... | collective-permute-start | bytes 196616 | tf_op jit(solution)/shard_map/ppermute | solution.py:43
  57.5 1.3 collective-permute-start.7
  59.4 4.3 %collective-permute-done.7 = f32[64,2,128]{2,0,1:T(8,128)S(1)} collective-permute-done((f32[64,2,128]{2,0,1:T(8,128)S(1)}, f32[64,2,128]{2,0,1:T(8,128)S(1)}, u32[]{:S(2)}, u32[]{:S(2)}) %collective-permute-start.7) | collective-permute-done | bytes 65568 | tf_op jit(solution)/shard_map/ppermute | solution.py:44
  64.2 1.2 add_multiply_fusion
  65.8 2.0 fusion.8
  67.9 69.9 %psum.21 = f32[1024]{0:T(1024)S(1)} all-reduce(f32[1024]{0:T(1024)S(1)} %get-tuple-element.5), channel_id=1, replica_groups=mesh['mod'=4,'frm'=2,'ori'=4] {'frm'}, use_global_device_ids=true, to_apply=%region_1.0 | all-reduce | flops 1024 | bytes 8192 | tf_op jit(solution)/shard_map/psum | solution.py:83
  137.7 7.4 %pad_maximum_fusion = bf16[2,1,1024,16,128]{4,3,0,2,1:T(8,128)(2,1)} fusion(bf16[1,1,1024,16,128]{4,3,0,2,1:T(8,128)(2,1)} %bitcast.3, bf16[1,1,1024,16,128]{4,3,0,2,1:T(8,128)(2,1)} %get-tuple-element.7), kind=kLoop, calls=%fused_computation.1 | loop fusion | flops 4194304 | bytes 16777216 | tf_op jit(solution)/shard_map/stack | solution.py:26
  145.2 11.1 %reverse_select_fusion = bf16[2,1,1024,16,128]{4,3,0,2,1:T(8,128)(2,1)} fusion(bf16[2,1,1024,16,128]{4,3,0,2,1:T(8,128)(2,1)} %pad_maximum_fusion, pred[]{:T(512)S(6)} %eq.3), kind=kLoop, calls=%fused_computation | loop fusion | flops 4194304 | bytes 16777216 | tf_op jit(solution)/shard_map/jit(_where)/select_n | solution.py:28
  156.3 9.6 %fusion.5 = f32[256,1024]{1,0:T(8,128)} fusion(bf16[256,32,128]{2,0,1:T(8,128)(2,1)} %all-gather.2.cloned.1.call-done, bf16[1024,32,128]{2,1,0:T(8,128)(2,1)} %bitcast.19, f32[1024]{0:T(1024)S(1)} %psum.21), kind=kOutput, calls=%fused_computation.7 | convolution fusion | flops 2147745792 | bytes 11538432 | tf_op jit(solution)/shard_map/dot_general | solution.py:84
  166.0 52.1 %all-reduce.18.cloned.1.call-done = f32[256,1024]{1,0:T(8,128)} async-done(((f32[256,1024]{1,0:T(8,128)}), f32[256,1024]{1,0:T(8,128)}) %all-reduce.18.cloned.1.call-update) | async-done | bytes 1048592 | tf_op jit(solution)/shard_map/psum | solution.py:92
  218.0 1.1 fusion.9
  219.1 6.9 %pmax.7 = f32[64]{0:T(128)S(1)} all-reduce(f32[64]{0:T(128)S(1)} %fusion.9), channel_id=1, replica_groups=mesh['mod'=4,'frm'=2,'ori'=4] {'ori'}, use_global_device_ids=true, to_apply=%region_4.5 | all-reduce | flops 64 | bytes 512 | tf_op jit(solution)/shard_map/pmax | solution.py:96
  226.0 1.2 exponential_reduce_fusion
  227.1 5.9 %psum.23 = f32[64]{0:T(128)S(1)} all-reduce(f32[64]{0:T(128)S(1)} %exponential_reduce_fusion), channel_id=1, replica_groups=mesh['mod'=4,'frm'=2,'ori'=4] {'ori'}, use_global_device_ids=true, to_apply=%region_6.7 | all-reduce | flops 64 | bytes 512 | tf_op jit(solution)/shard_map/psum | solution.py:97
  233.1 1.7 subtract_bitcast_fusion
  (38 shorter events, 5.4 us)
Async XLA Ops:
  6.5 149.8 %all-gather.2.cloned.1.call-start = ((), (), s32[]{:S(2)}) async-start(), calls=%async_computation | async-start | bytes 2621440 | tf_op jit(solution)/shard_map/all_gather | solution.py:76
  8.4 6.9 %collective-permute-start = (f32[64,2,128]{2,0,1:T(8,128)S(1)}, f32[64,2,128]{2,0,1:T(8,128)S(1)}, u32[]{:S(2)}, u32[]{:S(2)}) collective-permute-start(f32[64,2,128]{2,0,1:T(8,128)S(1)} %get-tuple-element.30), channel_id=1, source_target_pairs={{0,8},{8,16},{16,24},{1,9},{9,17},{17,25},{2,10},{10,18},{18,26},{... | collective-permute-start | bytes 196616 | tf_op jit(solution)/shard_map/ppermute | solution.py:43
  13.4 6.2 %collective-permute-start.1 = (f32[64,2,128]{2,0,1:T(8,128)S(1)}, f32[64,2,128]{2,0,1:T(8,128)S(1)}, u32[]{:S(2)}, u32[]{:S(2)}) collective-permute-start(f32[64,2,128]{2,0,1:T(8,128)S(1)} %get-tuple-element.31), channel_id=1, source_target_pairs={{8,0},{16,8},{24,16},{9,1},{17,9},{25,17},{10,2},{18,10},{26,18},{... | collective-permute-start | bytes 196616 | tf_op jit(solution)/shard_map/ppermute | solution.py:44
  21.6 5.9 %copy-start = (s32[32,128]{1,0:T(8,128)S(1)}, s32[32,128]{1,0:T(8,128)}, u32[]{:S(2)}) copy-start(s32[32,128]{1,0:T(8,128)} %param.5) | copy-start | bytes 49156
  22.8 5.4 %collective-permute-start.2 = (f32[64,2,128]{2,0,1:T(8,128)S(1)}, f32[64,2,128]{2,0,1:T(8,128)S(1)}, u32[]{:S(2)}, u32[]{:S(2)}) collective-permute-start(f32[64,2,128]{2,0,1:T(8,128)S(1)} %get-tuple-element.28), channel_id=1, source_target_pairs={{0,8},{8,16},{16,24},{1,9},{9,17},{17,25},{2,10},{10,18},{18,26},{... | collective-permute-start | bytes 196616 | tf_op jit(solution)/shard_map/ppermute | solution.py:43
  26.3 6.2 %collective-permute-start.3 = (f32[64,2,128]{2,0,1:T(8,128)S(1)}, f32[64,2,128]{2,0,1:T(8,128)S(1)}, u32[]{:S(2)}, u32[]{:S(2)}) collective-permute-start(f32[64,2,128]{2,0,1:T(8,128)S(1)} %get-tuple-element.29), channel_id=1, source_target_pairs={{8,0},{16,8},{24,16},{9,1},{17,9},{25,17},{10,2},{18,10},{26,18},{... | collective-permute-start | bytes 196616 | tf_op jit(solution)/shard_map/ppermute | solution.py:44
  32.9 7.8 %slice-start = ((s8[8388608]{0:T(1024)(128)(4,1)}), s8[4194304]{0:T(1024)(128)(4,1)S(1)}, s32[]{:S(2)}) async-start(s8[8388608]{0:T(1024)(128)(4,1)} %bitcast.20), calls=%async_computation.2 | async-start | bytes 8388608
  34.2 6.5 %slice-start.1 = ((s8[8388608]{0:T(1024)(128)(4,1)}), s8[4194304]{0:T(1024)(128)(4,1)S(1)}, s32[]{:S(2)}) async-start(s8[8388608]{0:T(1024)(128)(4,1)} %bitcast.20), calls=%async_computation.3 | async-start | bytes 8388608
  35.7 14.0 %collective-permute-start.4 = (f32[64,2,128]{2,0,1:T(8,128)S(1)}, f32[64,2,128]{2,0,1:T(8,128)S(1)}, u32[]{:S(2)}, u32[]{:S(2)}) collective-permute-start(f32[64,2,128]{2,0,1:T(8,128)S(1)} %get-tuple-element.26), channel_id=1, source_target_pairs={{0,8},{8,16},{16,24},{1,9},{9,17},{17,25},{2,10},{10,18},{18,26},{... | collective-permute-start | bytes 196616 | tf_op jit(solution)/shard_map/ppermute | solution.py:43
  39.2 10.5 %collective-permute-start.5 = (f32[64,2,128]{2,0,1:T(8,128)S(1)}, f32[64,2,128]{2,0,1:T(8,128)S(1)}, u32[]{:S(2)}, u32[]{:S(2)}) collective-permute-start(f32[64,2,128]{2,0,1:T(8,128)S(1)} %get-tuple-element.27), channel_id=1, source_target_pairs={{8,0},{16,8},{24,16},{9,1},{17,9},{25,17},{10,2},{18,10},{26,18},{... | collective-permute-start | bytes 196616 | tf_op jit(solution)/shard_map/ppermute | solution.py:44
  48.2 89.5 %collective-permute-start.8 = (bf16[1,1024,16,128]{3,2,1,0:T(8,128)(2,1)}, bf16[1,1024,16,128]{3,2,1,0:T(8,128)(2,1)}, u32[]{:S(2)}, u32[]{:S(2)}) collective-permute-start(bf16[1,1024,16,128]{3,2,1,0:T(8,128)(2,1)} %get-tuple-element.6), channel_id=1, source_target_pairs={{0,4},{4,0},{1,5},{5,1},{2,6},{6,2},{3,7},{7,3},{8,12},{12,8},{9,1... | collective-permute-start | bytes 12582920 | tf_op jit(solution)/shard_map/ppermute | solution.py:25
  52.9 6.4 %collective-permute-start.6 = (f32[64,2,128]{2,0,1:T(8,128)S(1)}, f32[64,2,128]{2,0,1:T(8,128)S(1)}, u32[]{:S(2)}, u32[]{:S(2)}) collective-permute-start(f32[64,2,128]{2,0,1:T(8,128)S(1)} %get-tuple-element.24), channel_id=1, source_target_pairs={{0,8},{8,16},{16,24},{1,9},{9,17},{17,25},{2,10},{10,18},{18,26},{... | collective-permute-start | bytes 196616 | tf_op jit(solution)/shard_map/ppermute | solution.py:43
  57.5 6.2 %collective-permute-start.7 = (f32[64,2,128]{2,0,1:T(8,128)S(1)}, f32[64,2,128]{2,0,1:T(8,128)S(1)}, u32[]{:S(2)}, u32[]{:S(2)}) collective-permute-start(f32[64,2,128]{2,0,1:T(8,128)S(1)} %get-tuple-element.25), channel_id=1, source_target_pairs={{8,0},{16,8},{24,16},{9,1},{17,9},{25,17},{10,2},{18,10},{26,18},{... | collective-permute-start | bytes 196616 | tf_op jit(solution)/shard_map/ppermute | solution.py:44
  67.8 150.2 %all-reduce.18.cloned.1.call-start = ((), (), s32[]{:S(2)}) async-start(), calls=%async_computation.1 | async-start | bytes 2097152 | tf_op jit(solution)/shard_map/psum | solution.py:92
Sparse Core Ops, SparseCore 0:
  67.9 19.8 all-gather.1
  166.1 51.9 all-reduce.17
